TPU v7x, 32 devices: a whole 2x2x4 slice. The times are simulated.
32 devices in a mesh: row: 4 (over y, core), blk: 8 (over z, x).
Axes of the slice: x: 2, y: 2, z: 4, core: 2. Of those that a mesh axis runs over, the one named last changes fastest.
Arguments:
- right_side: float32 [4, 8, 8, 32, 256], P('row', 'blk')
- noise_level: float32 [4, 8, 8, 256], P('row', 'blk'), may hold values from 3 to 6
- near_blocks: bfloat16 [4, 8, 8, 9, 256, 256], P('row', 'blk'), as said below
- skeleton_basis: bfloat16 [4, 8, 8, 64, 256], P('row', 'blk'), may hold values from -0.125 to 0.125
- skeleton_index: int32 [4, 8, 64], P('row', 'blk'), may hold values from 0 to 2047, as said below
- far_list: int32 [4, 8, 7], P('row', 'blk'), may hold values from 0 to 7, as said below
- couplings: bfloat16 [4, 8, 7, 64, 64], P('row', 'blk'), as said below
Outputs:
- solution: float32 [4, 8, 8, 32, 256], P('row', 'blk')
- residual: float32 [4, 8, 8, 32, 256], P('row', 'blk')
- quadratic: float32 [32], replicated
Inputs may be any that keep to these rules, and one draw needn't show every extreme that they name: `far_list`: each device's 7 entries are distinct, none is the device's own blk index, and the two cyclic neighbours along blk are always among them; box b lists box b' exactly when b' lists b, and within a row every box's far boxes lie at the same set of cyclic offsets from its own index. `couplings`: the coupling that box b holds for far box b' is the transpose of the one that b' holds for b. `near_blocks`: A leaf's block for near slot s is the transpose of the block that its slot-s neighbour holds for slot 8 - s; slot 4 blocks are symmetric. `skeleton_index`: each device's 64 entries are distinct tracers of its 2048.
All inputs are finite; a program needn't handle non-finite values.
Results may differ from a plain program's by a relative error of at most 0.03.
Values may be sent and summed in bfloat16 or wider, within the bound.
A program may use at most 64 MiB of HBM per device.

v0:
```python
import jax
import jax.numpy as jnp
from jax import lax
from jax.sharding import PartitionSpec as P

ITERS = 4
LEAF_ROWS = 2
LEAF_COLS = 4


def extended_2(array, sides, width):
    for axis, dim in sides:
        count, length = (lax.axis_size(axis), array.shape[dim])
        up = [(i, (i + 1) % count) for i in range(count)]
        down = [(j, i) for i, j in up]
        last = lax.slice_in_dim(array, length - width, length, axis=dim)
        leading = lax.slice_in_dim(array, 0, width, axis=dim)
        before = lax.ppermute(last, axis, up)
        after = lax.ppermute(leading, axis, down)
        array = jnp.concatenate([before, array, after], axis=dim)
    return array


def local(
    right_side, noise_level, near_blocks, skeleton_basis, skeleton_index, far_list, couplings
):
    local_noise = noise_level[0, 0][:, None, :]
    leaf_count = near_blocks.shape[2]
    width = near_blocks.shape[4]
    blocks_grid = near_blocks[0, 0].reshape(LEAF_ROWS, LEAF_COLS, 9, width, width)
    basis_local = skeleton_basis[0, 0]
    skeleton_local = skeleton_index[0, 0]
    far_local = far_list[0, 0]
    coupling_local = couplings[0, 0]
    points = basis_local.shape[2]
    owner_leaf = skeleton_local // points
    owner_point = skeleton_local % points

    def column_sum(values):
        return jnp.sum(values, axis=(0, 1, 2, 4))

    def residual_sum(values):
        return lax.psum(column_sum(values * values), ("row", "blk"))

    solution = jnp.zeros_like(right_side)
    residual = right_side
    direction = right_side
    norm_now = residual_sum(residual)
    for step_index in range(ITERS):
        rounded = direction.astype(jnp.bfloat16)
        own_field = rounded[0, 0]
        columns = own_field.shape[1]
        leaf_grid = own_field.reshape(LEAF_ROWS, LEAF_COLS, columns, width)
        extended = extended_2(leaf_grid, (("row", 0), ("blk", 1)), 1)
        sources = jnp.stack(
            [
                extended[slot // 3 : slot // 3 + LEAF_ROWS, slot % 3 : slot % 3 + LEAF_COLS]
                for slot in range(9)
            ],
            axis=2,
        )
        near = jnp.einsum(
            "abkci,abkij->abcj", sources, blocks_grid, preferred_element_type=jnp.float32
        )
        result = near.reshape(leaf_count, columns, width)
        picked = own_field[owner_leaf, :, owner_point].astype(jnp.float32)
        skeleton = picked.T + jnp.einsum(
            "lci,lki->ck", own_field, basis_local, preferred_element_type=jnp.float32
        )
        all_skeletons = lax.all_gather(
            skeleton.astype(jnp.bfloat16)[None], "blk", axis=0, tiled=True
        )
        selected = all_skeletons[far_local]
        far_sum = jnp.einsum(
            "jck,jkm->cm", selected, coupling_local, preferred_element_type=jnp.float32
        )
        result = result + jnp.einsum(
            "ck,lki->lci",
            far_sum.astype(jnp.bfloat16),
            basis_local,
            preferred_element_type=jnp.float32,
        )
        result = result.at[owner_leaf, :, owner_point].add(far_sum.T)
        applied = (local_noise * direction[0, 0] + result)[None, None]
        curve = lax.psum(column_sum(direction * applied), ("row", "blk"))
        step_size = norm_now / curve
        solution = solution + step_size[:, None] * direction
        residual = residual - step_size[:, None] * applied
        norm_next = residual_sum(residual)
        direction = residual + (norm_next / norm_now)[:, None] * direction
        norm_now = norm_next
    total = lax.psum(column_sum(right_side * solution), ("row", "blk"))
    tracer_count = (
        lax.axis_size("row") * lax.axis_size("blk") * right_side.shape[2] * right_side.shape[4]
    )
    quadratic = total / tracer_count
    return (solution, residual, quadratic)


def solution(mesh):
    return jax.shard_map(
        local,
        mesh=mesh,
        in_specs=(
            P("row", "blk", None, None, None),
            P("row", "blk", None, None),
            P("row", "blk", None, None, None, None),
            P("row", "blk", None, None, None),
            P("row", "blk", None),
            P("row", "blk", None),
            P("row", "blk", None, None, None),
        ),
        out_specs=(P("row", "blk", None, None, None), P("row", "blk", None, None, None), P()),
        check_vma=False,
    )
```

profile of v0, /device:TPU:0, one launch (start us, length us, event | category | flops | bytes accessed | tf_op | source)
XLA Modules:
  0.0 537.6 jit_solution(16591721626279821936)
XLA Ops:
  5.8 30.8 %all-gather = bf16[256,64]{1,0:T(8,128)(2,1)S(1)} all-gather(bf16[32,64]{1,0:T(8,128)(2,1)S(1)} %fusion.12), channel_id=2, replica_groups=mesh['row'=4,'blk'=8] {'blk'}, dimensions={0}, use_global_device_ids=true | all-gather | bytes 36864 | tf_op jit(solution)/shard_map/all_gather | solution.py:70
  37.3 4.2 collective-permute-start.3
  43.5 5.1 collective-permute-done.2
  48.8 5.4 %fusion.95 = f32[2,4,32,256,1]{3,2,4,1,0:T(8,128)S(1)} fusion(bf16[2,4,9,32,256]{4,3,2,1,0:T(8,128)(2,1)S(1)} %fusion.58, bf16[2,4,9,256,256]{4,3,2,1,0:T(8,128)(2,1)} %bitcast.461), kind=kOutput, calls=%fused_computation.214 | convolution fusion | flops 301989888 | bytes 10878976 | tf_op jit(solution)/shard_map/abkci,abkij->abcj/dot_general | solution.py:62
  54.7 3.7 scatter_fusion
  59.0 36.9 %all-reduce = (f32[32]{0:T(128)S(1)}, f32[32]{0:T(128)S(1)}) all-reduce(f32[32]{0:T(128)S(1)} %get-tuple-element.32, f32[32]{0:T(128)S(1)} %fusion.16), channel_id=1, replica_groups=mesh['row'=4,'blk'=8] {'row','blk'}, use_global_device_ids=true, to_apply=%region_1.2 | all-reduce | flops 64 | bytes 512 | tf_op jit(solution)/shard_map/psum | solution.py:43
  96.1 42.0 %psum.65 = f32[32]{0:T(128)S(1)} all-reduce(f32[32]{0:T(128)S(1)} %multiply_reduce_fusion.3), channel_id=1, replica_groups=mesh['row'=4,'blk'=8] {'row','blk'}, use_global_device_ids=true, to_apply=%region_6.7 | all-reduce | flops 32 | bytes 256 | tf_op jit(solution)/shard_map/psum | solution.py:43
  140.2 30.6 %all-gather.1 = bf16[256,64]{1,0:T(8,128)(2,1)S(1)} all-gather(bf16[32,64]{1,0:T(8,128)(2,1)S(1)} %fusion.13), channel_id=3, replica_groups=mesh['row'=4,'blk'=8] {'blk'}, dimensions={0}, use_global_device_ids=true | all-gather | bytes 36864 | tf_op jit(solution)/shard_map/all_gather | solution.py:70
  176.5 5.1 collective-permute-done.6
  181.8 5.4 %fusion.96 = f32[2,4,32,256,1]{3,2,4,1,0:T(8,128)S(1)} fusion(bf16[2,4,9,32,256]{4,3,2,1,0:T(8,128)(2,1)S(1)} %fusion.48, bf16[2,4,9,256,256]{4,3,2,1,0:T(8,128)(2,1)} %bitcast.462), kind=kOutput, calls=%fused_computation.215 | convolution fusion | flops 301989888 | bytes 10878976 | tf_op jit(solution)/shard_map/abkci,abkij->abcj/dot_general | solution.py:62
  191.8 36.9 %psum.66 = f32[32]{0:T(128)S(1)} all-reduce(f32[32]{0:T(128)S(1)} %fusion.19), channel_id=1, replica_groups=mesh['row'=4,'blk'=8] {'row','blk'}, use_global_device_ids=true, to_apply=%region_9.10 | all-reduce | flops 32 | bytes 256 | tf_op jit(solution)/shard_map/psum | solution.py:85
  229.0 41.7 %psum.67 = f32[32]{0:T(128)S(1)} all-reduce(f32[32]{0:T(128)S(1)} %get-tuple-element.13), channel_id=1, replica_groups=mesh['row'=4,'blk'=8] {'row','blk'}, use_global_device_ids=true, to_apply=%region_11.12 | all-reduce | flops 32 | bytes 256 | tf_op jit(solution)/shard_map/psum | solution.py:43
  272.9 30.5 %all-gather.2 = bf16[256,64]{1,0:T(8,128)(2,1)S(1)} all-gather(bf16[32,64]{1,0:T(8,128)(2,1)S(1)} %fusion.14), channel_id=4, replica_groups=mesh['row'=4,'blk'=8] {'blk'}, dimensions={0}, use_global_device_ids=true | all-gather | bytes 36864 | tf_op jit(solution)/shard_map/all_gather | solution.py:70
  309.2 5.1 collective-permute-done.10
  314.5 5.4 %fusion.97 = f32[2,4,32,256,1]{3,2,4,1,0:T(8,128)S(1)} fusion(bf16[2,4,9,32,256]{4,3,2,1,0:T(8,128)(2,1)S(1)} %fusion.38, bf16[2,4,9,256,256]{4,3,2,1,0:T(8,128)(2,1)} %bitcast.463), kind=kOutput, calls=%fused_computation.216 | convolution fusion | flops 301989888 | bytes 10878976 | tf_op jit(solution)/shard_map/abkci,abkij->abcj/dot_general | solution.py:62
  320.4 3.7 scatter_fusion.2
  324.5 36.9 %psum.68 = f32[32]{0:T(128)S(1)} all-reduce(f32[32]{0:T(128)S(1)} %fusion.18), channel_id=1, replica_groups=mesh['row'=4,'blk'=8] {'row','blk'}, use_global_device_ids=true, to_apply=%region_14.15 | all-reduce | flops 32 | bytes 256 | tf_op jit(solution)/shard_map/psum | solution.py:85
  361.6 42.0 %psum.69 = f32[32]{0:T(128)S(1)} all-reduce(f32[32]{0:T(128)S(1)} %get-tuple-element.9), channel_id=1, replica_groups=mesh['row'=4,'blk'=8] {'row','blk'}, use_global_device_ids=true, to_apply=%region_16.17 | all-reduce | flops 32 | bytes 256 | tf_op jit(solution)/shard_map/psum | solution.py:43
  405.7 30.6 %all-gather.3 = bf16[256,64]{1,0:T(8,128)(2,1)S(1)} all-gather(bf16[32,64]{1,0:T(8,128)(2,1)S(1)} %fusion.15), channel_id=5, replica_groups=mesh['row'=4,'blk'=8] {'blk'}, dimensions={0}, use_global_device_ids=true | all-gather | bytes 36864 | tf_op jit(solution)/shard_map/all_gather | solution.py:70
  442.0 5.1 collective-permute-done.14
  447.3 5.4 %fusion.98 = f32[2,4,32,256,1]{3,2,4,1,0:T(8,128)S(1)} fusion(bf16[2,4,9,32,256]{4,3,2,1,0:T(8,128)(2,1)S(1)} %fusion.28, bf16[2,4,9,256,256]{4,3,2,1,0:T(8,128)(2,1)} %bitcast.464), kind=kOutput, calls=%fused_computation.217 | convolution fusion | flops 301989888 | bytes 10878976 | tf_op jit(solution)/shard_map/abkci,abkij->abcj/dot_general | solution.py:62
  453.3 3.7 scatter_fusion.3
  457.4 36.9 %psum.70 = f32[32]{0:T(128)S(1)} all-reduce(f32[32]{0:T(128)S(1)} %fusion.17), channel_id=1, replica_groups=mesh['row'=4,'blk'=8] {'row','blk'}, use_global_device_ids=true, to_apply=%region_19.20 | all-reduce | flops 32 | bytes 256 | tf_op jit(solution)/shard_map/psum | solution.py:85
  495.3 41.7 %psum.71 = f32[32]{0:T(128)S(1)} all-reduce(f32[32]{0:T(128)S(1)} %get-tuple-element.5), channel_id=1, replica_groups=mesh['row'=4,'blk'=8] {'row','blk'}, use_global_device_ids=true, to_apply=%region_21.22 | all-reduce | flops 32 | bytes 256 | tf_op jit(solution)/shard_map/psum | solution.py:92
  (153 shorter events, 41.6 us)
Async XLA Ops:
  0.6 5.0 copy-start
  0.6 4.0 copy-start.4
  0.7 36.0 %copy-start.5 = (s32[1,1,7]{2,1,0:T(1,128)S(1)}, s32[1,1,7]{2,1,0:T(1,128)}, u32[]{:S(2)}) copy-start(s32[1,1,7]{2,1,0:T(1,128)} %param.12) | copy-start | bytes 88
  0.7 40.9 %copy-start.2 = (bf16[1,1,7,64,64]{4,3,2,1,0:T(8,128)(2,1)S(1)}, bf16[1,1,7,64,64]{4,3,2,1,0:T(8,128)(2,1)}, u32[]{:S(2)}) copy-start(bf16[1,1,7,64,64]{4,3,2,1,0:T(8,128)(2,1)} %param.13) | copy-start | bytes 172036
  1.9 39.9 %copy-start.1 = (f32[1,1,8,32,256]{4,3,2,1,0:T(8,128)S(1)}, f32[1,1,8,32,256]{4,3,2,1,0:T(8,128)}, u32[]{:S(2)}) copy-start(f32[1,1,8,32,256]{4,3,2,1,0:T(8,128)} %param.7) | copy-start | bytes 786436
  1.9 35.3 %collective-permute-start.1 = (bf16[1,4,32,256]{3,2,1,0:T(8,128)(2,1)S(1)}, bf16[1,4,32,256]{3,2,1,0:T(8,128)(2,1)S(1)}, u32[]{:S(2)}, u32[]{:S(2)}) collective-permute-start(bf16[1,4,32,256]{3,2,1,0:T(8,128)(2,1)S(1)} %get-tuple-element.45), channel_id=1, source_target_pairs={{8,0},{16,8},{24,16},{0,24},{9,1},{17,9},{25,17},{1,25},{10,2},{18... | collective-permute-start | bytes 196616 | tf_op jit(solution)/shard_map/ppermute | solution.py:19
  4.4 32.9 %collective-permute-start = (bf16[1,4,32,256]{3,2,1,0:T(8,128)(2,1)S(1)}, bf16[1,4,32,256]{3,2,1,0:T(8,128)(2,1)S(1)}, u32[]{:S(2)}, u32[]{:S(2)}) collective-permute-start(bf16[1,4,32,256]{3,2,1,0:T(8,128)(2,1)S(1)} %get-tuple-element.44), channel_id=1, source_target_pairs={{0,8},{8,16},{16,24},{24,0},{1,9},{9,17},{17,25},{25,1},{2,10},{10... | collective-permute-start | bytes 196616 | tf_op jit(solution)/shard_map/ppermute | solution.py:18
  37.3 6.1 %collective-permute-start.3 = (bf16[4,1,32,256]{3,2,1,0:T(8,128)(2,1)S(1)}, bf16[4,1,32,256]{3,2,1,0:T(8,128)(2,1)S(1)}, u32[]{:S(2)}, u32[]{:S(2)}) collective-permute-start(bf16[4,1,32,256]{3,2,1,0:T(8,128)(2,1)S(1)} %get-tuple-element.36), channel_id=1, source_target_pairs={{1,0},{2,1},{3,2},{4,3},{5,4},{6,5},{7,6},{0,7},{9,8},{10,9},{11,1... | collective-permute-start | bytes 196616 | tf_op jit(solution)/shard_map/ppermute | solution.py:19
  41.5 7.0 %collective-permute-start.2 = (bf16[4,1,32,256]{3,2,1,0:T(8,128)(2,1)S(1)}, bf16[4,1,32,256]{3,2,1,0:T(8,128)(2,1)S(1)}, u32[]{:S(2)}, u32[]{:S(2)}) collective-permute-start(bf16[4,1,32,256]{3,2,1,0:T(8,128)(2,1)S(1)} %get-tuple-element.37), channel_id=1, source_target_pairs={{0,1},{1,2},{2,3},{3,4},{4,5},{5,6},{6,7},{7,0},{8,9},{9,10},{10,1... | collective-permute-start | bytes 196616 | tf_op jit(solution)/shard_map/ppermute | solution.py:18
  48.7 5.4 %copy-start.3 = (f32[1,1,8,256]{3,2,1,0:T(8,128)S(1)}, f32[1,1,8,256]{3,2,1,0:T(8,128)}, u32[]{:S(2)}) copy-start(f32[1,1,8,256]{3,2,1,0:T(8,128)} %param.8) | copy-start | bytes 24580
  138.2 33.1 %collective-permute-start.5 = (bf16[1,4,32,256]{3,2,1,0:T(8,128)(2,1)S(1)}, bf16[1,4,32,256]{3,2,1,0:T(8,128)(2,1)S(1)}, u32[]{:S(2)}, u32[]{:S(2)}) collective-permute-start(bf16[1,4,32,256]{3,2,1,0:T(8,128)(2,1)S(1)} %get-tuple-element.43), channel_id=1, source_target_pairs={{8,0},{16,8},{24,16},{0,24},{9,1},{17,9},{25,17},{1,25},{10,2},{18... | collective-permute-start | bytes 196616 | tf_op jit(solution)/shard_map/ppermute | solution.py:19
  138.6 32.7 %collective-permute-start.4 = (bf16[1,4,32,256]{3,2,1,0:T(8,128)(2,1)S(1)}, bf16[1,4,32,256]{3,2,1,0:T(8,128)(2,1)S(1)}, u32[]{:S(2)}, u32[]{:S(2)}) collective-permute-start(bf16[1,4,32,256]{3,2,1,0:T(8,128)(2,1)S(1)} %get-tuple-element.42), channel_id=1, source_target_pairs={{0,8},{8,16},{16,24},{24,0},{1,9},{9,17},{17,25},{25,1},{2,10},{10... | collective-permute-start | bytes 196616 | tf_op jit(solution)/shard_map/ppermute | solution.py:18
  171.4 5.2 collective-permute-start.7
  174.6 7.0 %collective-permute-start.6 = (bf16[4,1,32,256]{3,2,1,0:T(8,128)(2,1)S(1)}, bf16[4,1,32,256]{3,2,1,0:T(8,128)(2,1)S(1)}, u32[]{:S(2)}, u32[]{:S(2)}) collective-permute-start(bf16[4,1,32,256]{3,2,1,0:T(8,128)(2,1)S(1)} %get-tuple-element.31), channel_id=1, source_target_pairs={{0,1},{1,2},{2,3},{3,4},{4,5},{5,6},{6,7},{7,0},{8,9},{9,10},{10,1... | collective-permute-start | bytes 196616 | tf_op jit(solution)/shard_map/ppermute | solution.py:18
  270.8 33.2 %collective-permute-start.9 = (bf16[1,4,32,256]{3,2,1,0:T(8,128)(2,1)S(1)}, bf16[1,4,32,256]{3,2,1,0:T(8,128)(2,1)S(1)}, u32[]{:S(2)}, u32[]{:S(2)}) collective-permute-start(bf16[1,4,32,256]{3,2,1,0:T(8,128)(2,1)S(1)} %get-tuple-element.41), channel_id=1, source_target_pairs={{8,0},{16,8},{24,16},{0,24},{9,1},{17,9},{25,17},{1,25},{10,2},{18... | collective-permute-start | bytes 196616 | tf_op jit(solution)/shard_map/ppermute | solution.py:19
  271.5 32.5 %collective-permute-start.8 = (bf16[1,4,32,256]{3,2,1,0:T(8,128)(2,1)S(1)}, bf16[1,4,32,256]{3,2,1,0:T(8,128)(2,1)S(1)}, u32[]{:S(2)}, u32[]{:S(2)}) collective-permute-start(bf16[1,4,32,256]{3,2,1,0:T(8,128)(2,1)S(1)} %get-tuple-element.40), channel_id=1, source_target_pairs={{0,8},{8,16},{16,24},{24,0},{1,9},{9,17},{17,25},{25,1},{2,10},{10... | collective-permute-start | bytes 196616 | tf_op jit(solution)/shard_map/ppermute | solution.py:18
  304.1 5.1 collective-permute-start.11
  307.3 7.0 %collective-permute-start.10 = (bf16[4,1,32,256]{3,2,1,0:T(8,128)(2,1)S(1)}, bf16[4,1,32,256]{3,2,1,0:T(8,128)(2,1)S(1)}, u32[]{:S(2)}, u32[]{:S(2)}) collective-permute-start(bf16[4,1,32,256]{3,2,1,0:T(8,128)(2,1)S(1)} %get-tuple-element.27), channel_id=1, source_target_pairs={{0,1},{1,2},{2,3},{3,4},{4,5},{5,6},{6,7},{7,0},{8,9},{9,10},{10,1... | collective-permute-start | bytes 196616 | tf_op jit(solution)/shard_map/ppermute | solution.py:18
  403.7 33.1 %collective-permute-start.13 = (bf16[1,4,32,256]{3,2,1,0:T(8,128)(2,1)S(1)}, bf16[1,4,32,256]{3,2,1,0:T(8,128)(2,1)S(1)}, u32[]{:S(2)}, u32[]{:S(2)}) collective-permute-start(bf16[1,4,32,256]{3,2,1,0:T(8,128)(2,1)S(1)} %get-tuple-element.39), channel_id=1, source_target_pairs={{8,0},{16,8},{24,16},{0,24},{9,1},{17,9},{25,17},{1,25},{10,2},{18... | collective-permute-start | bytes 196616 | tf_op jit(solution)/shard_map/ppermute | solution.py:19
  404.1 32.8 %collective-permute-start.12 = (bf16[1,4,32,256]{3,2,1,0:T(8,128)(2,1)S(1)}, bf16[1,4,32,256]{3,2,1,0:T(8,128)(2,1)S(1)}, u32[]{:S(2)}, u32[]{:S(2)}) collective-permute-start(bf16[1,4,32,256]{3,2,1,0:T(8,128)(2,1)S(1)} %get-tuple-element.38), channel_id=1, source_target_pairs={{0,8},{8,16},{16,24},{24,0},{1,9},{9,17},{17,25},{25,1},{2,10},{10... | collective-permute-start | bytes 196616 | tf_op jit(solution)/shard_map/ppermute | solution.py:18
  436.9 5.1 collective-permute-start.15
  440.1 7.0 %collective-permute-start.14 = (bf16[4,1,32,256]{3,2,1,0:T(8,128)(2,1)S(1)}, bf16[4,1,32,256]{3,2,1,0:T(8,128)(2,1)S(1)}, u32[]{:S(2)}, u32[]{:S(2)}) collective-permute-start(bf16[4,1,32,256]{3,2,1,0:T(8,128)(2,1)S(1)} %get-tuple-element.23), channel_id=1, source_target_pairs={{0,1},{1,2},{2,3},{3,4},{4,5},{5,6},{6,7},{7,0},{8,9},{9,10},{10,1... | collective-permute-start | bytes 196616 | tf_op jit(solution)/shard_map/ppermute | solution.py:18
where the time goes:
time: 539 us; the launch traced here: 538 us
  blocking collectives  438 us (81%)
  waiting for transfers between devices  26.4 us (5%)
  matrix products  23.9 us (4%)
  other arithmetic  19.6 us (4%)
  starting transfers between devices  18.2 us (3%)
  local copies, waits for them, and re-layouts  10.6 us (2%)
    psum x4, blocking collectives, residual_sum(): return lax.psum(column_sum(values * values), ('row', 'blk'))  163 us
    all_gather x4, blocking collectives, local(): lax.all_gather(skeleton.astype(jnp.bfloat16)[None], 'blk', axis=0, tiled=...  123 us
    psum x3, blocking collectives, local(): curve = lax.psum(column_sum(direction * applied), ('row', 'blk'))  111 us
    psum x1, blocking collectives, local(): total = lax.psum(column_sum(right_side * solution), ('row', 'blk'))  41.7 us
    dot_general x4, matrix products, local(): jnp.einsum('abkci,abkij->abcj', sources, blocks_grid, preferred_element_t...  21.6 us
    ppermute x8, waiting for transfers between devices, extended_2(): before = lax.ppermute(last, axis, up)  20.2 us
    ppermute x8, starting transfers between devices, extended_2(): after = lax.ppermute(leading, axis, down)  17.8 us
    scatter-add x4, other arithmetic, local(): result = result.at[owner_leaf, :, owner_point].add(far_sum.T)  14.7 us
  transfers between devices with their start and end apart: 16, of which 8 were waited for; matrix products, arithmetic and copies ran while one was open for 2% of the time, Pallas kernels for 0%

commit v1 on v0

--- a/solution.py
+++ b/solution.py
@@ -67,9 +67,25 @@
         skeleton = picked.T + jnp.einsum(
             "lci,lki->ck", own_field, basis_local, preferred_element_type=jnp.float32
         )
-        all_skeletons = lax.all_gather(
-            skeleton.astype(jnp.bfloat16)[None], "blk", axis=0, tiled=True
-        )
+        value = skeleton.astype(jnp.bfloat16)[None]
+        size, index, rows = (lax.axis_size("blk"), lax.axis_index("blk"), value.shape[0])
+        right = [(i_2, (i_2 + 1) % size) for i_2 in range(size)]
+        downward = [(i_2, (i_2 - 1) % size) for i_2 in range(size)]
+        whole = jnp.zeros((*value.shape[:0], size * rows, *value.shape[0 + 1 :]), value.dtype)
+        whole = lax.dynamic_update_slice_in_dim(whole, value, index * rows, axis=0)
+        from_left = from_right = value
+        middle = size // 2
+        for lap in range(1, middle + 1):
+            from_left = lax.ppermute(from_left, "blk", right)
+            whole = lax.dynamic_update_slice_in_dim(
+                whole, from_left, (index - lap) % size * rows, axis=0
+            )
+            if lap < size - middle:
+                from_right = lax.ppermute(from_right, "blk", downward)
+                whole = lax.dynamic_update_slice_in_dim(
+                    whole, from_right, (index + lap) % size * rows, axis=0
+                )
+        all_skeletons = whole
         selected = all_skeletons[far_local]
         far_sum = jnp.einsum(
             "jck,jkm->cm", selected, coupling_local, preferred_element_type=jnp.float32

time: 539 us -> 507 us (0.941)
  blocking collectives: 438 us -> 320 us
  starting transfers between devices: 18.2 us -> 69.4 us
  waiting for transfers between devices: 26.4 us -> 60.1 us
    all_gather x4 -> x0, blocking collectives: 123 us -> none  [local(): lax.all_gather(skeleton.astype(jnp.bfloat16)[None], 'blk', axis=0, tiled=...]
    ppermute x0 -> x28, starting transfers between devices: none -> 58.8 us  [the longest x12 48.8 us: local(): from_right = lax.ppermute(from_right, 'blk', downward)]
    ppermute x0 -> x28, waiting for transfers between devices: none -> 41.2 us  [the longest x16 41.1 us: local(): from_left = lax.ppermute(from_left, 'blk', right)]
    ppermute x8, starting transfers between devices: 17.8 us -> 0.97 us  [extended_2(): after = lax.ppermute(leading, axis, down)]
    ppermute x8, starting transfers between devices: 0.4 us -> 9.58 us  [extended_2(): before = lax.ppermute(last, axis, up)]
    ppermute x8, waiting for transfers between devices: 20.2 us -> 11.1 us  [extended_2(): before = lax.ppermute(last, axis, up)]
  transfers between devices with their start and end apart: 16 -> 44, of which waited for: 8 -> 24; matrix products, arithmetic and copies ran while one was open for 2% -> 1% of each run, Pallas kernels for 0% -> 0%
where the time goes in v1:
time: 507 us; the launch traced here: 506 us
  blocking collectives  320 us (63%)
  starting transfers between devices  69.4 us (14%)
  waiting for transfers between devices  60.1 us (12%)
  matrix products  23.9 us (5%)
  other arithmetic  20.3 us (4%)
  local copies, waits for them, and re-layouts  10.9 us (2%)
    psum x4, blocking collectives, residual_sum(): return lax.psum(column_sum(values * values), ('row', 'blk'))  165 us
    psum x3, blocking collectives, local(): curve = lax.psum(column_sum(direction * applied), ('row', 'blk'))  112 us
    ppermute x12, starting transfers between devices, local(): from_right = lax.ppermute(from_right, 'blk', downward)  48.8 us
    psum x1, blocking collectives, local(): total = lax.psum(column_sum(right_side * solution), ('row', 'blk'))  42.9 us
    ppermute x16, waiting for transfers between devices, local(): from_left = lax.ppermute(from_left, 'blk', right)  41.1 us
    dot_general x4, matrix products, local(): jnp.einsum('abkci,abkij->abcj', sources, blocks_grid, preferred_element_t...  21.6 us
    scatter-add x4, other arithmetic, local(): result = result.at[owner_leaf, :, owner_point].add(far_sum.T)  14.7 us
    ppermute x8, waiting for transfers between devices, extended_2(): before = lax.ppermute(last, axis, up)  11.1 us
  transfers between devices with their start and end apart: 44, of which 24 were waited for; matrix products, arithmetic and copies ran while one was open for 1% of the time, Pallas kernels for 0%

profile of v1, /device:TPU:0, one launch (start us, length us, event | category | flops | bytes accessed | tf_op | source)
XLA Modules:
  0.0 505.8 jit_solution(8675629429856396640)
XLA Ops:
  11.7 4.8 collective-permute-start.7
  18.1 4.8 collective-permute-start.9
  24.4 6.3 %collective-permute-done.10 = bf16[1,32,64]{2,1,0:T(8,128)(2,1)S(1)} collective-permute-done((bf16[1,32,64]{2,1,0:T(8,128)(2,1)S(1)}, bf16[1,32,64]{2,1,0:T(8,128)(2,1)S(1)}, u32[]{:S(2)}, u32[]{:S(2)}) %collective-permute-start.10) | collective-permute-done | bytes 4128 | tf_op jit(solution)/shard_map/ppermute | solution.py:79
  38.7 5.4 %fusion.99 = f32[2,4,32,256,1]{3,2,4,1,0:T(8,128)S(1)} fusion(bf16[2,4,9,32,256]{4,3,2,1,0:T(8,128)(2,1)S(1)} %fusion.62, bf16[2,4,9,256,256]{4,3,2,1,0:T(8,128)(2,1)} %bitcast.489), kind=kOutput, calls=%fused_computation.250 | convolution fusion | flops 301989888 | bytes 10878976 | tf_op jit(solution)/shard_map/abkci,abkij->abcj/dot_general | solution.py:62
  48.9 37.0 %all-reduce = (f32[32]{0:T(128)S(1)}, f32[32]{0:T(128)S(1)}) all-reduce(f32[32]{0:T(128)S(1)} %get-tuple-element.32, f32[32]{0:T(128)S(1)} %fusion.20), channel_id=1, replica_groups=mesh['row'=4,'blk'=8] {'row','blk'}, use_global_device_ids=true, to_apply=%region_1.2 | all-reduce | flops 64 | bytes 512 | tf_op jit(solution)/shard_map/psum | solution.py:43
  86.1 42.5 %psum.65 = f32[32]{0:T(128)S(1)} all-reduce(f32[32]{0:T(128)S(1)} %multiply_reduce_fusion.3), channel_id=1, replica_groups=mesh['row'=4,'blk'=8] {'row','blk'}, use_global_device_ids=true, to_apply=%region_6.7 | all-reduce | flops 32 | bytes 256 | tf_op jit(solution)/shard_map/psum | solution.py:43
  136.6 4.8 collective-permute-start.18
  142.9 4.8 collective-permute-start.20
  149.3 6.3 %collective-permute-done.21 = bf16[1,32,64]{2,1,0:T(8,128)(2,1)S(1)} collective-permute-done((bf16[1,32,64]{2,1,0:T(8,128)(2,1)S(1)}, bf16[1,32,64]{2,1,0:T(8,128)(2,1)S(1)}, u32[]{:S(2)}, u32[]{:S(2)}) %collective-permute-start.21) | collective-permute-done | bytes 4128 | tf_op jit(solution)/shard_map/ppermute | solution.py:79
  163.5 5.4 %fusion.100 = f32[2,4,32,256,1]{3,2,4,1,0:T(8,128)S(1)} fusion(bf16[2,4,9,32,256]{4,3,2,1,0:T(8,128)(2,1)S(1)} %fusion.52, bf16[2,4,9,256,256]{4,3,2,1,0:T(8,128)(2,1)} %bitcast.490), kind=kOutput, calls=%fused_computation.251 | convolution fusion | flops 301989888 | bytes 10878976 | tf_op jit(solution)/shard_map/abkci,abkij->abcj/dot_general | solution.py:62
  173.6 37.3 %psum.66 = f32[32]{0:T(128)S(1)} all-reduce(f32[32]{0:T(128)S(1)} %fusion.23), channel_id=1, replica_groups=mesh['row'=4,'blk'=8] {'row','blk'}, use_global_device_ids=true, to_apply=%region_9.10 | all-reduce | flops 32 | bytes 256 | tf_op jit(solution)/shard_map/psum | solution.py:101
  211.2 42.9 %psum.67 = f32[32]{0:T(128)S(1)} all-reduce(f32[32]{0:T(128)S(1)} %get-tuple-element.13), channel_id=1, replica_groups=mesh['row'=4,'blk'=8] {'row','blk'}, use_global_device_ids=true, to_apply=%region_11.12 | all-reduce | flops 32 | bytes 256 | tf_op jit(solution)/shard_map/psum | solution.py:43
  262.0 4.8 collective-permute-start.29
  268.3 4.8 collective-permute-start.31
  274.7 6.3 %collective-permute-done.32 = bf16[1,32,64]{2,1,0:T(8,128)(2,1)S(1)} collective-permute-done((bf16[1,32,64]{2,1,0:T(8,128)(2,1)S(1)}, bf16[1,32,64]{2,1,0:T(8,128)(2,1)S(1)}, u32[]{:S(2)}, u32[]{:S(2)}) %collective-permute-start.32) | collective-permute-done | bytes 4128 | tf_op jit(solution)/shard_map/ppermute | solution.py:79
  288.9 5.4 %fusion.101 = f32[2,4,32,256,1]{3,2,4,1,0:T(8,128)S(1)} fusion(bf16[2,4,9,32,256]{4,3,2,1,0:T(8,128)(2,1)S(1)} %fusion.42, bf16[2,4,9,256,256]{4,3,2,1,0:T(8,128)(2,1)} %bitcast.491), kind=kOutput, calls=%fused_computation.252 | convolution fusion | flops 301989888 | bytes 10878976 | tf_op jit(solution)/shard_map/abkci,abkij->abcj/dot_general | solution.py:62
  299.0 37.2 %psum.68 = f32[32]{0:T(128)S(1)} all-reduce(f32[32]{0:T(128)S(1)} %fusion.22), channel_id=1, replica_groups=mesh['row'=4,'blk'=8] {'row','blk'}, use_global_device_ids=true, to_apply=%region_14.15 | all-reduce | flops 32 | bytes 256 | tf_op jit(solution)/shard_map/psum | solution.py:101
  336.4 42.9 %psum.69 = f32[32]{0:T(128)S(1)} all-reduce(f32[32]{0:T(128)S(1)} %get-tuple-element.9), channel_id=1, replica_groups=mesh['row'=4,'blk'=8] {'row','blk'}, use_global_device_ids=true, to_apply=%region_16.17 | all-reduce | flops 32 | bytes 256 | tf_op jit(solution)/shard_map/psum | solution.py:43
  387.2 4.8 collective-permute-start.40
  393.6 4.8 collective-permute-start.42
  399.9 6.3 %collective-permute-done.43 = bf16[1,32,64]{2,1,0:T(8,128)(2,1)S(1)} collective-permute-done((bf16[1,32,64]{2,1,0:T(8,128)(2,1)S(1)}, bf16[1,32,64]{2,1,0:T(8,128)(2,1)S(1)}, u32[]{:S(2)}, u32[]{:S(2)}) %collective-permute-start.43) | collective-permute-done | bytes 4128 | tf_op jit(solution)/shard_map/ppermute | solution.py:79
  414.2 5.4 %fusion.102 = f32[2,4,32,256,1]{3,2,4,1,0:T(8,128)S(1)} fusion(bf16[2,4,9,32,256]{4,3,2,1,0:T(8,128)(2,1)S(1)} %fusion.32, bf16[2,4,9,256,256]{4,3,2,1,0:T(8,128)(2,1)} %bitcast.492), kind=kOutput, calls=%fused_computation.253 | convolution fusion | flops 301989888 | bytes 10878976 | tf_op jit(solution)/shard_map/abkci,abkij->abcj/dot_general | solution.py:62
  424.2 37.2 %psum.70 = f32[32]{0:T(128)S(1)} all-reduce(f32[32]{0:T(128)S(1)} %fusion.21), channel_id=1, replica_groups=mesh['row'=4,'blk'=8] {'row','blk'}, use_global_device_ids=true, to_apply=%region_19.20 | all-reduce | flops 32 | bytes 256 | tf_op jit(solution)/shard_map/psum | solution.py:101
  462.4 42.9 %psum.71 = f32[32]{0:T(128)S(1)} all-reduce(f32[32]{0:T(128)S(1)} %get-tuple-element.5), channel_id=1, replica_groups=mesh['row'=4,'blk'=8] {'row','blk'}, use_global_device_ids=true, to_apply=%region_21.22 | all-reduce | flops 32 | bytes 256 | tf_op jit(solution)/shard_map/psum | solution.py:108
  (235 shorter events, 99.5 us)
Async XLA Ops:
  4.1 7.7 %collective-permute-start.4 = (bf16[1,32,64]{2,1,0:T(8,128)(2,1)S(1)}, bf16[1,32,64]{2,1,0:T(8,128)(2,1)S(1)}, u32[]{:S(2)}, u32[]{:S(2)}) collective-permute-start(bf16[1,32,64]{2,1,0:T(8,128)(2,1)S(1)} %get-tuple-element.48), channel_id=1, source_target_pairs={{0,1},{1,2},{2,3},{3,4},{4,5},{5,6},{6,7},{7,0},{8,9},{9,10},{10,1... | collective-permute-start | bytes 12296 | tf_op jit(solution)/shard_map/ppermute | solution.py:79
  10.2 21.2 %collective-permute-start.1 = (bf16[1,4,32,256]{3,2,1,0:T(8,128)(2,1)S(1)}, bf16[1,4,32,256]{3,2,1,0:T(8,128)(2,1)S(1)}, u32[]{:S(2)}, u32[]{:S(2)}) collective-permute-start(bf16[1,4,32,256]{3,2,1,0:T(8,128)(2,1)S(1)} %get-tuple-element.45), channel_id=1, source_target_pairs={{8,0},{16,8},{24,16},{0,24},{9,1},{17,9},{25,17},{1,25},{10,2},{18... | collective-permute-start | bytes 196616 | tf_op jit(solution)/shard_map/ppermute | solution.py:19
  10.9 20.5 %collective-permute-start = (bf16[1,4,32,256]{3,2,1,0:T(8,128)(2,1)S(1)}, bf16[1,4,32,256]{3,2,1,0:T(8,128)(2,1)S(1)}, u32[]{:S(2)}, u32[]{:S(2)}) collective-permute-start(bf16[1,4,32,256]{3,2,1,0:T(8,128)(2,1)S(1)} %get-tuple-element.44), channel_id=1, source_target_pairs={{0,8},{8,16},{16,24},{24,0},{1,9},{9,17},{17,25},{25,1},{2,10},{10... | collective-permute-start | bytes 196616 | tf_op jit(solution)/shard_map/ppermute | solution.py:18
  11.7 6.3 %collective-permute-start.6 = (bf16[1,32,64]{2,1,0:T(8,128)(2,1)S(1)}, bf16[1,32,64]{2,1,0:T(8,128)(2,1)S(1)}, u32[]{:S(2)}, u32[]{:S(2)}) collective-permute-start(bf16[1,32,64]{2,1,0:T(8,128)(2,1)S(1)} %collective-permute-done.4), channel_id=1, source_target_pairs={{0,1},{1,2},{2,3},{3,4},{4,5},{5,6},{6,7},{7,0},{8,9},{9,10},{10,1... | collective-permute-start | bytes 12296 | tf_op jit(solution)/shard_map/ppermute | solution.py:79
  18.1 6.3 %collective-permute-start.8 = (bf16[1,32,64]{2,1,0:T(8,128)(2,1)S(1)}, bf16[1,32,64]{2,1,0:T(8,128)(2,1)S(1)}, u32[]{:S(2)}, u32[]{:S(2)}) collective-permute-start(bf16[1,32,64]{2,1,0:T(8,128)(2,1)S(1)} %collective-permute-done.6), channel_id=1, source_target_pairs={{0,1},{1,2},{2,3},{3,4},{4,5},{5,6},{6,7},{7,0},{8,9},{9,10},{10,1... | collective-permute-start | bytes 12296 | tf_op jit(solution)/shard_map/ppermute | solution.py:79
  18.1 6.4 %collective-permute-start.9 = (bf16[1,32,64]{2,1,0:T(8,128)(2,1)S(1)}, bf16[1,32,64]{2,1,0:T(8,128)(2,1)S(1)}, u32[]{:S(2)}, u32[]{:S(2)}) collective-permute-start(bf16[1,32,64]{2,1,0:T(8,128)(2,1)S(1)} %collective-permute-done.7), channel_id=1, source_target_pairs={{0,7},{1,0},{2,1},{3,2},{4,3},{5,4},{6,5},{7,6},{8,15},{9,8},{10,9... | collective-permute-start | bytes 12296 | tf_op jit(solution)/shard_map/ppermute | solution.py:84
  24.4 6.3 %collective-permute-start.10 = (bf16[1,32,64]{2,1,0:T(8,128)(2,1)S(1)}, bf16[1,32,64]{2,1,0:T(8,128)(2,1)S(1)}, u32[]{:S(2)}, u32[]{:S(2)}) collective-permute-start(bf16[1,32,64]{2,1,0:T(8,128)(2,1)S(1)} %collective-permute-done.8), channel_id=1, source_target_pairs={{0,1},{1,2},{2,3},{3,4},{4,5},{5,6},{6,7},{7,0},{8,9},{9,10},{10,1... | collective-permute-start | bytes 12296 | tf_op jit(solution)/shard_map/ppermute | solution.py:79
  31.4 7.0 %collective-permute-start.2 = (bf16[4,1,32,256]{3,2,1,0:T(8,128)(2,1)S(1)}, bf16[4,1,32,256]{3,2,1,0:T(8,128)(2,1)S(1)}, u32[]{:S(2)}, u32[]{:S(2)}) collective-permute-start(bf16[4,1,32,256]{3,2,1,0:T(8,128)(2,1)S(1)} %get-tuple-element.37), channel_id=1, source_target_pairs={{0,1},{1,2},{2,3},{3,4},{4,5},{5,6},{6,7},{7,0},{8,9},{9,10},{10,1... | collective-permute-start | bytes 196616 | tf_op jit(solution)/shard_map/ppermute | solution.py:18
  130.2 6.4 %collective-permute-start.15 = (bf16[1,32,64]{2,1,0:T(8,128)(2,1)S(1)}, bf16[1,32,64]{2,1,0:T(8,128)(2,1)S(1)}, u32[]{:S(2)}, u32[]{:S(2)}) collective-permute-start(bf16[1,32,64]{2,1,0:T(8,128)(2,1)S(1)} %get-tuple-element.50), channel_id=1, source_target_pairs={{0,1},{1,2},{2,3},{3,4},{4,5},{5,6},{6,7},{7,0},{8,9},{9,10},{10,1... | collective-permute-start | bytes 12296 | tf_op jit(solution)/shard_map/ppermute | solution.py:79
  135.0 21.2 %collective-permute-start.12 = (bf16[1,4,32,256]{3,2,1,0:T(8,128)(2,1)S(1)}, bf16[1,4,32,256]{3,2,1,0:T(8,128)(2,1)S(1)}, u32[]{:S(2)}, u32[]{:S(2)}) collective-permute-start(bf16[1,4,32,256]{3,2,1,0:T(8,128)(2,1)S(1)} %get-tuple-element.43), channel_id=1, source_target_pairs={{8,0},{16,8},{24,16},{0,24},{9,1},{17,9},{25,17},{1,25},{10,2},{18... | collective-permute-start | bytes 196616 | tf_op jit(solution)/shard_map/ppermute | solution.py:19
  135.0 21.2 %collective-permute-start.11 = (bf16[1,4,32,256]{3,2,1,0:T(8,128)(2,1)S(1)}, bf16[1,4,32,256]{3,2,1,0:T(8,128)(2,1)S(1)}, u32[]{:S(2)}, u32[]{:S(2)}) collective-permute-start(bf16[1,4,32,256]{3,2,1,0:T(8,128)(2,1)S(1)} %get-tuple-element.42), channel_id=1, source_target_pairs={{0,8},{8,16},{16,24},{24,0},{1,9},{9,17},{17,25},{25,1},{2,10},{10... | collective-permute-start | bytes 196616 | tf_op jit(solution)/shard_map/ppermute | solution.py:18
  136.6 6.3 %collective-permute-start.18 = (bf16[1,32,64]{2,1,0:T(8,128)(2,1)S(1)}, bf16[1,32,64]{2,1,0:T(8,128)(2,1)S(1)}, u32[]{:S(2)}, u32[]{:S(2)}) collective-permute-start(bf16[1,32,64]{2,1,0:T(8,128)(2,1)S(1)} %collective-permute-done.16), channel_id=1, source_target_pairs={{0,7},{1,0},{2,1},{3,2},{4,3},{5,4},{6,5},{7,6},{8,15},{9,8},{10,9... | collective-permute-start | bytes 12296 | tf_op jit(solution)/shard_map/ppermute | solution.py:84
  142.9 6.3 %collective-permute-start.20 = (bf16[1,32,64]{2,1,0:T(8,128)(2,1)S(1)}, bf16[1,32,64]{2,1,0:T(8,128)(2,1)S(1)}, u32[]{:S(2)}, u32[]{:S(2)}) collective-permute-start(bf16[1,32,64]{2,1,0:T(8,128)(2,1)S(1)} %collective-permute-done.18), channel_id=1, source_target_pairs={{0,7},{1,0},{2,1},{3,2},{4,3},{5,4},{6,5},{7,6},{8,15},{9,8},{10,9... | collective-permute-start | bytes 12296 | tf_op jit(solution)/shard_map/ppermute | solution.py:84
  156.3 7.0 %collective-permute-start.13 = (bf16[4,1,32,256]{3,2,1,0:T(8,128)(2,1)S(1)}, bf16[4,1,32,256]{3,2,1,0:T(8,128)(2,1)S(1)}, u32[]{:S(2)}, u32[]{:S(2)}) collective-permute-start(bf16[4,1,32,256]{3,2,1,0:T(8,128)(2,1)S(1)} %get-tuple-element.31), channel_id=1, source_target_pairs={{0,1},{1,2},{2,3},{3,4},{4,5},{5,6},{6,7},{7,0},{8,9},{9,10},{10,1... | collective-permute-start | bytes 196616 | tf_op jit(solution)/shard_map/ppermute | solution.py:18
  255.6 6.4 %collective-permute-start.26 = (bf16[1,32,64]{2,1,0:T(8,128)(2,1)S(1)}, bf16[1,32,64]{2,1,0:T(8,128)(2,1)S(1)}, u32[]{:S(2)}, u32[]{:S(2)}) collective-permute-start(bf16[1,32,64]{2,1,0:T(8,128)(2,1)S(1)} %get-tuple-element.52), channel_id=1, source_target_pairs={{0,1},{1,2},{2,3},{3,4},{4,5},{5,6},{6,7},{7,0},{8,9},{9,10},{10,1... | collective-permute-start | bytes 12296 | tf_op jit(solution)/shard_map/ppermute | solution.py:79
  260.4 21.2 %collective-permute-start.23 = (bf16[1,4,32,256]{3,2,1,0:T(8,128)(2,1)S(1)}, bf16[1,4,32,256]{3,2,1,0:T(8,128)(2,1)S(1)}, u32[]{:S(2)}, u32[]{:S(2)}) collective-permute-start(bf16[1,4,32,256]{3,2,1,0:T(8,128)(2,1)S(1)} %get-tuple-element.41), channel_id=1, source_target_pairs={{8,0},{16,8},{24,16},{0,24},{9,1},{17,9},{25,17},{1,25},{10,2},{18... | collective-permute-start | bytes 196616 | tf_op jit(solution)/shard_map/ppermute | solution.py:19
  260.4 21.2 %collective-permute-start.22 = (bf16[1,4,32,256]{3,2,1,0:T(8,128)(2,1)S(1)}, bf16[1,4,32,256]{3,2,1,0:T(8,128)(2,1)S(1)}, u32[]{:S(2)}, u32[]{:S(2)}) collective-permute-start(bf16[1,4,32,256]{3,2,1,0:T(8,128)(2,1)S(1)} %get-tuple-element.40), channel_id=1, source_target_pairs={{0,8},{8,16},{16,24},{24,0},{1,9},{9,17},{17,25},{25,1},{2,10},{10... | collective-permute-start | bytes 196616 | tf_op jit(solution)/shard_map/ppermute | solution.py:18
  262.0 6.3 %collective-permute-start.28 = (bf16[1,32,64]{2,1,0:T(8,128)(2,1)S(1)}, bf16[1,32,64]{2,1,0:T(8,128)(2,1)S(1)}, u32[]{:S(2)}, u32[]{:S(2)}) collective-permute-start(bf16[1,32,64]{2,1,0:T(8,128)(2,1)S(1)} %collective-permute-done.26), channel_id=1, source_target_pairs={{0,1},{1,2},{2,3},{3,4},{4,5},{5,6},{6,7},{7,0},{8,9},{9,10},{10,1... | collective-permute-start | bytes 12296 | tf_op jit(solution)/shard_map/ppermute | solution.py:79
  262.0 6.3 %collective-permute-start.29 = (bf16[1,32,64]{2,1,0:T(8,128)(2,1)S(1)}, bf16[1,32,64]{2,1,0:T(8,128)(2,1)S(1)}, u32[]{:S(2)}, u32[]{:S(2)}) collective-permute-start(bf16[1,32,64]{2,1,0:T(8,128)(2,1)S(1)} %collective-permute-done.27), channel_id=1, source_target_pairs={{0,7},{1,0},{2,1},{3,2},{4,3},{5,4},{6,5},{7,6},{8,15},{9,8},{10,9... | collective-permute-start | bytes 12296 | tf_op jit(solution)/shard_map/ppermute | solution.py:84
  281.7 7.0 %collective-permute-start.24 = (bf16[4,1,32,256]{3,2,1,0:T(8,128)(2,1)S(1)}, bf16[4,1,32,256]{3,2,1,0:T(8,128)(2,1)S(1)}, u32[]{:S(2)}, u32[]{:S(2)}) collective-permute-start(bf16[4,1,32,256]{3,2,1,0:T(8,128)(2,1)S(1)} %get-tuple-element.27), channel_id=1, source_target_pairs={{0,1},{1,2},{2,3},{3,4},{4,5},{5,6},{6,7},{7,0},{8,9},{9,10},{10,1... | collective-permute-start | bytes 196616 | tf_op jit(solution)/shard_map/ppermute | solution.py:18
  380.8 6.4 %collective-permute-start.37 = (bf16[1,32,64]{2,1,0:T(8,128)(2,1)S(1)}, bf16[1,32,64]{2,1,0:T(8,128)(2,1)S(1)}, u32[]{:S(2)}, u32[]{:S(2)}) collective-permute-start(bf16[1,32,64]{2,1,0:T(8,128)(2,1)S(1)} %get-tuple-element.54), channel_id=1, source_target_pairs={{0,1},{1,2},{2,3},{3,4},{4,5},{5,6},{6,7},{7,0},{8,9},{9,10},{10,1... | collective-permute-start | bytes 12296 | tf_op jit(solution)/shard_map/ppermute | solution.py:79
  385.6 21.2 %collective-permute-start.34 = (bf16[1,4,32,256]{3,2,1,0:T(8,128)(2,1)S(1)}, bf16[1,4,32,256]{3,2,1,0:T(8,128)(2,1)S(1)}, u32[]{:S(2)}, u32[]{:S(2)}) collective-permute-start(bf16[1,4,32,256]{3,2,1,0:T(8,128)(2,1)S(1)} %get-tuple-element.39), channel_id=1, source_target_pairs={{8,0},{16,8},{24,16},{0,24},{9,1},{17,9},{25,17},{1,25},{10,2},{18... | collective-permute-start | bytes 196616 | tf_op jit(solution)/shard_map/ppermute | solution.py:19
  385.6 21.2 %collective-permute-start.33 = (bf16[1,4,32,256]{3,2,1,0:T(8,128)(2,1)S(1)}, bf16[1,4,32,256]{3,2,1,0:T(8,128)(2,1)S(1)}, u32[]{:S(2)}, u32[]{:S(2)}) collective-permute-start(bf16[1,4,32,256]{3,2,1,0:T(8,128)(2,1)S(1)} %get-tuple-element.38), channel_id=1, source_target_pairs={{0,8},{8,16},{16,24},{24,0},{1,9},{9,17},{17,25},{25,1},{2,10},{10... | collective-permute-start | bytes 196616 | tf_op jit(solution)/shard_map/ppermute | solution.py:18
  406.9 7.0 %collective-permute-start.35 = (bf16[4,1,32,256]{3,2,1,0:T(8,128)(2,1)S(1)}, bf16[4,1,32,256]{3,2,1,0:T(8,128)(2,1)S(1)}, u32[]{:S(2)}, u32[]{:S(2)}) collective-permute-start(bf16[4,1,32,256]{3,2,1,0:T(8,128)(2,1)S(1)} %get-tuple-element.23), channel_id=1, source_target_pairs={{0,1},{1,2},{2,3},{3,4},{4,5},{5,6},{6,7},{7,0},{8,9},{9,10},{10,1... | collective-permute-start | bytes 196616 | tf_op jit(solution)/shard_map/ppermute | solution.py:18
  (25 other events, 169.0 us)
